TPU v7x, 768 devices: a whole 4x8x12 slice. The times are simulated.
768 devices in a mesh: rows: 64 (over z_hi, y, core), cols: 12 (over x, z_lo).
Axes of the slice: x: 4, y: 8, z: 12 (z_hi: 4, z_lo: 3; z = z_hi * 3 + z_lo), core: 2. Of those that a mesh axis runs over, the one named last changes fastest.
Arguments:
- values: bfloat16 [49152, 6144], P('rows', 'cols'), may hold values from -6 to 6
- tile_scale: float32 [192, 24], P('rows', 'cols'), may hold values from 0.1 to 10
- occupancy: int32 [192, 24], P('rows', 'cols'), may hold values from 0 to 1, as said below
- row_kind: int32 [49152], P('rows'), may hold values 0 or 1
- right_side: float32 [128, 49152], P(None, 'rows'), may hold values from -6 to 6
- cost_vector: float32 [128, 6144], P(None, 'cols'), may hold values from -6 to 6
- lower_bound: float32 [6144], P('cols'), may hold values from -2 to -0.2
- upper_bound: float32 [6144], P('cols'), may hold values from 0.2 to 2
- x_start: float32 [128, 6144], P(None, 'cols'), may hold values from -3 to 3
- y_start: float32 [128, 49152], P(None, 'rows'), may hold values from -3 to 3
- step_sizes: float32 [2], replicated, may hold values from 0.005 to 0.02
Outputs:
- x_next: float32 [128, 6144], P(None, 'cols')
- y_next: float32 [128, 49152], P(None, 'rows')
- measures: float32 [3, 128], replicated
- primal_move: float32 [128], replicated
Inputs may be any that keep to these rules, and one draw needn't show every extreme that they name: `occupancy`: every tile row and every tile column of 256 x 256 tiles holds at least one occupied tile.
All inputs are finite; a program needn't handle non-finite values. No bound on the sum of `row_kind` on one device may be relied on, other than what follows from the above.
Results may differ from a plain program's by a relative error of at most 0.00038.
Values sent between devices are 32-bit elements; how exact they have to be, the bound alone decides.
A program may use at most 32 MiB of HBM per device.

v0:
```python
import jax
import jax.numpy as jnp
from jax import lax
from jax.sharding import PartitionSpec as P

EPS = 1e-06


def forward_part(blocks, factor, vectors):
    scenario_count = vectors.shape[0]
    tile_rows, tile_width, tile_cols, _ = blocks.shape
    flattened = blocks.reshape(tile_rows * tile_width, tile_cols, tile_width)
    shaped = vectors.reshape(scenario_count, tile_cols, tile_width)
    pieces = jnp.einsum("ibj,sbj->sbi", flattened, shaped, preferred_element_type=jnp.float32)
    weight = jnp.repeat(factor.T, tile_width, axis=1)
    return jnp.sum(pieces * weight[None], axis=1)


def backward_part(blocks, factor, vectors):
    scenario_count = vectors.shape[0]
    tile_rows, tile_width, tile_cols, _ = blocks.shape
    shaped = vectors.reshape(scenario_count, tile_rows, tile_width)
    pieces = jnp.einsum("aibj,sai->sabj", blocks, shaped, preferred_element_type=jnp.float32)
    summed = jnp.einsum("sabj,ab->sbj", pieces, factor, precision=lax.Precision.HIGHEST)
    return summed.reshape(scenario_count, tile_cols * tile_width)


def dual_image(blocks, factor, vectors):
    partial_value = backward_part(blocks, factor, vectors)
    return lax.psum(partial_value, "rows")


def per_device(
    values,
    tile_scale,
    occupancy,
    row_kind,
    right_side,
    cost_vector,
    lower_bound,
    upper_bound,
    x_start,
    y_start,
    step_sizes,
):
    rows_here, cols_here = values.shape
    tile_rows, tile_cols = tile_scale.shape
    tile_width = rows_here // tile_rows
    factor = tile_scale * occupancy.astype(jnp.float32)
    blocks = values.reshape(tile_rows, tile_width, tile_cols, tile_width)
    magnitude = (jnp.abs(blocks).astype(jnp.float32) * factor[:, None, :, None]).reshape(
        rows_here, cols_here
    )
    row_scale = jnp.ones((rows_here,), jnp.float32)
    col_scale = jnp.ones((cols_here,), jnp.float32)
    for repeat_index in range(2):
        row_peak = jnp.max(magnitude * col_scale[None, :], axis=1)
        col_peak = jnp.max(magnitude * row_scale[:, None], axis=0)
        row_peak = lax.pmax(row_peak, "cols")
        col_peak = lax.pmax(col_peak, "rows")
        row_scale, col_scale = (
            row_scale / jnp.sqrt(row_scale * row_peak + EPS),
            col_scale / jnp.sqrt(col_scale * col_peak + EPS),
        )
    primal_step = step_sizes[0]
    dual_step = step_sizes[1]
    cost_scaled = cost_vector * col_scale[None]
    low_scaled = lower_bound / col_scale
    high_scaled = upper_bound / col_scale
    rhs_scaled = right_side * row_scale[None]
    dual_first = dual_image(blocks, factor, (y_start * row_scale[None]).astype(jnp.bfloat16))
    dual_first = col_scale[None] * dual_first
    x_next_part = jnp.clip(
        x_start - primal_step * (cost_scaled - dual_first), low_scaled[None], high_scaled[None]
    )
    first_input = (x_start * col_scale[None]).astype(jnp.bfloat16)
    next_input = (x_next_part * col_scale[None]).astype(jnp.bfloat16)
    first_terms = forward_part(blocks, factor, first_input)
    next_terms = forward_part(blocks, factor, next_input)
    image_first, image_next = lax.psum((first_terms, next_terms), "cols")
    image_first = row_scale[None] * image_first
    image_next = row_scale[None] * image_next
    inequality = (row_kind == 1)[None, :]
    dual_trial = y_start + dual_step * (rhs_scaled - (2.0 * image_next - image_first))
    y_next_part = jnp.where(inequality, jnp.maximum(dual_trial, 0.0), dual_trial)
    dual_second = col_scale[None] * dual_image(
        blocks, factor, (y_next_part * row_scale[None]).astype(jnp.bfloat16)
    )
    y_mean = 0.5 * (y_start + y_next_part)
    image_mean = 0.5 * (image_first + image_next)
    violation = rhs_scaled - image_mean
    violation = jnp.where(inequality, jnp.maximum(violation, 0.0), violation)
    y_terms = jnp.stack(
        [
            jnp.sum(violation * violation, axis=1),
            jnp.sum(rhs_scaled * y_mean, axis=1),
            jnp.sum((y_next_part - y_start) ** 2, axis=1),
        ]
    )
    reduced = cost_scaled - 0.5 * (dual_first + dual_second)
    x_mean = 0.5 * (x_start + x_next_part)
    bound_terms = low_scaled[None] * jnp.maximum(reduced, 0.0) - high_scaled[None] * jnp.maximum(
        -reduced, 0.0
    )
    x_terms = jnp.stack(
        [
            jnp.sum(cost_scaled * x_mean, axis=1),
            jnp.sum(bound_terms, axis=1),
            jnp.sum((x_next_part - x_start) ** 2, axis=1),
        ]
    )
    y_total = lax.psum(y_terms, "rows")
    x_total = lax.psum(x_terms, "cols")
    rows_total = rows_here * lax.axis_size("rows")
    cols_total = cols_here * lax.axis_size("cols")
    measures = jnp.stack(
        [
            y_total[0] / rows_total,
            (x_total[0] - y_total[1] - x_total[1]) / cols_total,
            y_total[2] / rows_total,
        ]
    )
    primal_move = x_total[2] / cols_total
    return (x_next_part, y_next_part, measures, primal_move)


def solution(mesh):
    return jax.shard_map(
        per_device,
        mesh=mesh,
        in_specs=(
            P("rows", "cols"),
            P("rows", "cols"),
            P("rows", "cols"),
            P("rows"),
            P(None, "rows"),
            P(None, "cols"),
            P("cols"),
            P("cols"),
            P(None, "cols"),
            P(None, "rows"),
            P(),
        ),
        out_specs=(P(None, "cols"), P(None, "rows"), P(), P()),
        check_vma=False,
    )
```

profile of v0, /device:TPU:1, one launch (start us, length us, event | category | flops | bytes accessed | tf_op | source)
XLA Modules:
  0.0 1566.2 jit_solution(12234977793483891056)
XLA Ops:
  7.2 0.0 all-reduce.5.cloned.1.call-start
  7.2 0.7 convert_multiply_fusion.1
  7.9 0.1 copy.31
  8.0 0.5 mul.170
  8.5 0.1 copy.56
  8.6 1.0 copy-done
  9.6 0.2 reshape.43
  9.8 0.8 fusion.18
  10.7 28.1 %pmax.29 = f32[768]{0:T(1024)S(1)} all-reduce(f32[768]{0:T(1024)S(1)} %get-tuple-element.10), channel_id=1, replica_groups=mesh['rows'=64,'cols'=12] {'cols'}, use_global_device_ids=true, to_apply=%region_3.0 | all-reduce | flops 768 | bytes 6144 | tf_op jit(solution)/shard_map/pmax | solution.py:59
  38.7 165.3 %pmax.28 = f32[512]{0:T(512)S(1)} all-reduce(f32[512]{0:T(512)} %get-tuple-element.11), channel_id=1, replica_groups=mesh['rows'=64,'cols'=12] {'rows'}, use_global_device_ids=true, to_apply=%region_1.0 | all-reduce | flops 512 | bytes 4096 | tf_op jit(solution)/shard_map/pmax | solution.py:60
  204.1 1.1 multiply_reduce_fusion.1
  205.2 21.0 %pmax.31 = f32[768]{0:T(1024)S(1)} all-reduce(f32[768]{0:T(1024)} %get-tuple-element.9), channel_id=1, replica_groups=mesh['rows'=64,'cols'=12] {'cols'}, use_global_device_ids=true, to_apply=%region_7.0 | all-reduce | flops 768 | bytes 6144 | tf_op jit(solution)/shard_map/pmax | solution.py:59
  226.3 0.2 copy.32
  226.4 0.3 convolution_bitcast_fusion.1
  226.7 0.0 copy-start.15
  226.8 0.0 copy-start.13
  226.8 0.0 copy-start.18
  226.8 0.0 copy-start.19
  226.8 2.1 fusion.4
  229.0 0.2 copy.45
  229.2 0.7 copy.57
  229.9 0.0 all-reduce.5.cloned.1.call-update
  229.9 0.0 all-reduce.9.cloned.1.call-start
  230.0 158.8 %pmax.30 = f32[512]{0:T(512)S(1)} all-reduce(f32[512]{0:T(512)S(1)} %copy-done.15), channel_id=1, replica_groups=mesh['rows'=64,'cols'=12] {'rows'}, use_global_device_ids=true, to_apply=%region_5.0 | all-reduce | flops 512 | bytes 4096 | tf_op jit(solution)/shard_map/pmax | solution.py:60
  388.8 0.1 broadcast_bitcast_fusion
  388.9 0.0 copy-start.10
  388.9 0.6 fusion.21
  389.5 419.0 %all-reduce.5.cloned.1.call-done = f32[128,512]{1,0:T(8,128)} async-done(((f32[128,512]{1,0:T(8,128)}), f32[128,512]{1,0:T(8,128)}) %all-reduce.5.cloned.1.call-update) | async-done | bytes 262160 | tf_op jit(solution)/shard_map/psum | solution.py:30
  808.5 1.7 multiply_convert_fusion.3
  810.3 1.1 fusion
  811.4 1.1 fusion.1
  812.6 0.0 all-reduce.9.cloned.1.call-update
  812.6 0.0 all-reduce.7.cloned.1.call-start
  812.7 127.3 %all-reduce.9.cloned.1.call-done = (f32[128,768]{1,0:T(8,128)}, f32[128,768]{1,0:T(8,128)}) async-done(((f32[128,768]{1,0:T(8,128)}, f32[128,768]{1,0:T(8,128)}), (f32[128,768]{1,0:T(8,128)}, f32[128,768]{1,0:T(8,128)})) %all-reduce.9.cloned.1.call-update) | async-done | bytes 786448 | tf_op jit(solution)/shard_map/psum | solution.py:80
  940.0 1.9 multiply_convert_fusion
  941.9 0.2 copy.39
  942.1 0.3 convolution_bitcast_fusion
  942.4 2.1 fusion.2
  944.6 0.2 copy.48
  944.8 0.7 copy.59
  945.5 0.0 all-reduce.7.cloned.1.call-update
  945.6 1.0 multiply_reduce_fusion.3
  946.6 160.9 %psum.45 = f32[3,128]{1,0:T(4,128)S(1)} all-reduce(f32[3,128]{1,0:T(4,128)S(1)} %pad_maximum_fusion), channel_id=1, replica_groups=mesh['rows'=64,'cols'=12] {'rows'}, use_global_device_ids=true, to_apply=%region_16.17 | all-reduce | flops 384 | bytes 3072 | tf_op jit(solution)/shard_map/psum | solution.py:112
  1107.4 426.2 %all-reduce.7.cloned.1.call-done = f32[128,512]{1,0:T(8,128)} async-done(((f32[128,512]{1,0:T(8,128)}), f32[128,512]{1,0:T(8,128)}) %all-reduce.7.cloned.1.call-update) | async-done | bytes 262160 | tf_op jit(solution)/shard_map/psum | solution.py:30
  1533.6 1.2 multiply_reduce_fusion.5
  1534.9 23.7 %psum.47 = f32[3,128]{1,0:T(4,128)S(1)} all-reduce(f32[3,128]{1,0:T(4,128)S(1)} %pad_maximum_fusion.1), channel_id=1, replica_groups=mesh['rows'=64,'cols'=12] {'cols'}, use_global_device_ids=true, to_apply=%region_21.22 | all-reduce | flops 384 | bytes 3072 | tf_op jit(solution)/shard_map/psum | solution.py:113
  1558.5 0.5 multiply_bitcast_fusion
  1559.1 0.6 pad_maximum_fusion.2
  (44 shorter events, 0.2 us)
Async XLA Ops:
  7.2 801.4 %all-reduce.5.cloned.1.call-start = ((), (), s32[]{:S(2)}) async-start(), calls=%async_computation | async-start | bytes 524288 | tf_op jit(solution)/shard_map/psum | solution.py:30
  8.5 1.1 copy-start
  10.6 215.6 %copy-start.1 = (f32[128,768]{1,0:T(8,128)S(1)}, f32[128,768]{1,0:T(8,128)}, u32[]{:S(2)}) copy-start(f32[128,768]{1,0:T(8,128)} %param.20) | copy-start | bytes 1179652
  204.1 1.1 copy-start.12
  226.7 3.3 copy-start.15
  226.8 162.1 %copy-start.13 = (f32[512]{0:T(512)S(1)}, f32[512]{0:T(512)}, u32[]{:S(2)}) copy-start(f32[512]{0:T(512)} %copy-done.12) | copy-start | bytes 6148
  226.8 162.1 %copy-start.17 = (f32[512]{0:T(512)S(1)}, f32[512]{0:T(512)}, u32[]{:S(2)}) copy-start(f32[512]{0:T(512)} %param.18) | copy-start | bytes 6148
  226.8 162.1 %copy-start.18 = (f32[512]{0:T(512)S(1)}, f32[512]{0:T(512)}, u32[]{:S(2)}) copy-start(f32[512]{0:T(512)} %param.17) | copy-start | bytes 6148
  226.8 162.1 %copy-start.19 = (f32[2]{0:T(128)S(1)}, f32[2]{0:T(128)}, u32[]{:S(2)}) copy-start(f32[2]{0:T(128)} %param.21) | copy-start | bytes 28
  226.8 581.7 %copy-start.6 = (f32[128,512]{1,0:T(8,128)S(1)}, f32[128,512]{1,0:T(8,128)}, u32[]{:S(2)}) copy-start(f32[128,512]{1,0:T(8,128)} %param.19) | copy-start | bytes 786436
  226.8 581.7 %copy-start.7 = (f32[128,512]{1,0:T(8,128)S(1)}, f32[128,512]{1,0:T(8,128)}, u32[]{:S(2)}) copy-start(f32[128,512]{1,0:T(8,128)} %param.16) | copy-start | bytes 786436
  229.9 710.0 %all-reduce.9.cloned.1.call-start = ((), (), s32[]{:S(2)}) async-start(), calls=%async_computation.2 | async-start | bytes 1572864 | tf_op jit(solution)/shard_map/psum | solution.py:80
  388.9 423.6 %copy-start.10 = (f32[512]{0:T(512)}, f32[512]{0:T(512)S(1)}, u32[]{:S(2)}) copy-start(f32[512]{0:T(512)S(1)} %div.30) | copy-start | bytes 6148
  810.2 723.4 %copy-start.8 = (f32[128,512]{1,0:T(8,128)}, f32[128,512]{1,0:T(8,128)S(1)}, u32[]{:S(2)}) copy-start(f32[128,512]{1,0:T(8,128)S(1)} %get-tuple-element.23) | copy-start | bytes 786436
  810.2 2.4 copy-start.16
  810.3 129.7 %copy-start.2 = (f32[128,768]{1,0:T(8,128)S(1)}, f32[128,768]{1,0:T(8,128)}, u32[]{:S(2)}) copy-start(f32[128,768]{1,0:T(8,128)} %param.15) | copy-start | bytes 1179652
  812.6 721.0 %all-reduce.7.cloned.1.call-start = ((), (), s32[]{:S(2)}) async-start(), calls=%async_computation.1 | async-start | bytes 524288 | tf_op jit(solution)/shard_map/psum | solution.py:30
  812.7 129.2 %copy-start.14 = (pred[768]{0:T(1024)(128)(4,1)}, pred[768]{0:T(1024)(128)(4,1)S(1)}, u32[]{:S(2)}) copy-start(pred[768]{0:T(1024)(128)(4,1)S(1)} %broadcast_compare_fusion) | copy-start | bytes 2308
  941.9 3.7 copy-start.3
  942.4 3.2 copy-start.4
  942.4 3.2 copy-start.5
  944.6 589.0 %copy-start.9 = (f32[128,512]{1,0:T(8,128)S(1)}, f32[128,512]{1,0:T(8,128)}, u32[]{:S(2)}) copy-start(f32[128,512]{1,0:T(8,128)} %all-reduce.5.cloned.1.call-done) | copy-start | bytes 786436
  944.6 589.0 %copy-start.11 = (f32[512]{0:T(512)S(1)}, f32[512]{0:T(512)}, u32[]{:S(2)}) copy-start(f32[512]{0:T(512)} %copy-done.10) | copy-start | bytes 6148
Sparse Core Ops, SparseCore 0:
  230.1 578.4 all-reduce.4
  812.7 127.2 all-reduce.8
  945.7 587.9 all-reduce.6
where the time goes:
time: 1580 us; the launch traced here: 1570 us
  waiting for transfers between devices  973 us (62%)
  blocking collectives  558 us (35%)
    psum x2, waiting for transfers between devices, dual_image(): return lax.psum(partial_value, 'rows')  845 us
    pmax x2, blocking collectives, per_device(): col_peak = lax.pmax(col_peak, 'rows')  324 us
    psum x1, blocking collectives, per_device(): y_total = lax.psum(y_terms, 'rows')  161 us
    psum x1, waiting for transfers between devices, per_device(): image_first, image_next = lax.psum((first_terms, next_terms), 'cols')  127 us
    pmax x2, blocking collectives, per_device(): row_peak = lax.pmax(row_peak, 'cols')  49.1 us
  transfers between devices with their start and end apart: 3, of which 3 were waited for; matrix products, arithmetic and copies ran while one was open for 0% of the time, Pallas kernels for 0%

commit v1 on v0

v1 whole, which is shorter than its diff:
```python
import jax
import jax.numpy as jnp
from jax import lax
from jax.experimental import pallas as pl
from jax.experimental.pallas import tpu as pltpu
from jax.sharding import PartitionSpec as P

EPS = 1e-06
MESH = pl.DeviceIdType.MESH
F32 = jnp.float32
BF16 = jnp.bfloat16

Z_HIGH, Y_SIZE, CORES = 4, 8, 2
X_SIZE, Z_LOW = 4, 3
LANE = 128
TILE = 256


def ring_distance(offset, size):
    return min(offset, size - offset)


def kernel(
    values_in,
    scale_ref,
    occupancy_ref,
    kind_ref,
    rhs_in,
    cost_in,
    low_ref,
    high_ref,
    x_in,
    y_in,
    step_ref,
    x_out,
    y_out,
    measures_ref,
    move_ref,
    values,
    rhs,
    cost,
    x_start,
    y_start,
    magnitude,
    col_peak,
    row_peak,
    col_first,
    row_first,
    col_second,
    col_scale,
    row_scale,
    part,
    half_in,
    half,
    group_in,
    high_slots,
    dual_first,
    x_full,
    image,
    image_in,
    image_first,
    y_full,
    y_sums,
    sums_cols,
    sums_rows,
    send,
    recv,
    local,
):
    scenarios = x_full.shape[0]
    rows_here, cols_here = values.shape
    row_blocks, col_blocks = rows_here // LANE, cols_here // LANE
    per_tile = TILE // LANE
    group_rows = scenarios // (CORES * Y_SIZE)
    half_rows = scenarios // CORES
    chunk_rows = scenarios // X_SIZE
    chunk_cols = rows_here // Z_LOW
    rows_total = float(rows_here * Z_HIGH * Y_SIZE * CORES)
    cols_total = float(cols_here * X_SIZE * Z_LOW)

    rank, column = lax.axis_index("rows"), lax.axis_index("cols")
    core = lax.rem(rank, CORES)
    y = lax.rem(lax.div(rank, CORES), Y_SIZE)
    z_high = lax.div(rank, CORES * Y_SIZE)
    x = lax.div(column, Z_LOW)
    z_low = lax.rem(column, Z_LOW)
    group = core * Y_SIZE + y

    def at_rows(z_at, y_at, core_at):
        return ((z_at * Y_SIZE + y_at) * CORES + core_at, column)

    def at_cols(x_at, low_at):
        return (rank, x_at * Z_LOW + low_at)

    def shift(index, offset, size):
        return lax.rem(index + offset + size, size)

    y_offsets = sorted(range(1, Y_SIZE), key=lambda k: -ring_distance(k, Y_SIZE))
    plane_offsets = [
        (dy, dc) for dy in range(Y_SIZE) for dc in range(CORES) if (dy, dc) != (0, 0)
    ]
    plane_offsets.sort(key=lambda o: -ring_distance(o[0], Y_SIZE))
    z_offsets = sorted(range(1, Z_HIGH), key=lambda k: -ring_distance(k, Z_HIGH))
    col_offsets = [
        (dx, dl) for dx in range(X_SIZE) for dl in range(Z_LOW) if (dx, dl) != (0, 0)
    ]
    col_offsets.sort(key=lambda o: -(ring_distance(o[0], X_SIZE) + (o[1] != 0)))

    def plane_at(offset, sign):
        return shift(y, sign * offset[0], Y_SIZE), shift(core, sign * offset[1], CORES)

    def cols_at(offset, sign):
        return shift(x, sign * offset[0], X_SIZE), shift(z_low, sign * offset[1], Z_LOW)

    plane_to = [at_rows(z_high, *plane_at(o, 1)) for o in plane_offsets]
    z_to = [at_rows(shift(z_high, k, Z_HIGH), y, core) for k in z_offsets]
    y_to = [at_rows(z_high, shift(y, k, Y_SIZE), core) for k in y_offsets]
    cols_to = [at_cols(*cols_at(o, 1)) for o in col_offsets]
    partner = at_rows(z_high, y, 1 - core)

    started = []
    used = [0]

    def reserve(count):
        base = used[0]
        used[0] += count
        return base

    def copy(source, target, slot, device):
        return pltpu.make_async_remote_copy(
            src_ref=source,
            dst_ref=target,
            send_sem=send.at[slot],
            recv_sem=recv.at[slot],
            device_id=device,
            device_id_type=MESH,
        )

    def put(source, target, slot, device):
        moved = copy(source, target, slot, device)
        moved.start()
        started.append(moved)

    def arrived(target, slot, device):
        copy(target, target, slot, device).wait_recv()

    def spread(source, slots, peers):
        base = reserve(len(peers))
        for k, device in enumerate(peers):
            put(source, slots.at[k], base + k, device)
        return base

    def collect(slots, base, peers):
        for k, device in enumerate(peers):
            arrived(slots.at[k], base + k, device)

    def block(index):
        return slice(index * LANE, (index + 1) * LANE)

    loads = [
        pltpu.make_async_copy(source, target, local.at[k])
        for k, (source, target) in enumerate(
            [(values_in, values), (y_in, y_start), (x_in, x_start), (cost_in, cost), (rhs_in, rhs)]
        )
    ]
    for load in loads:
        load.start()
    barrier = pltpu.get_barrier_semaphore()
    everyone = plane_to + z_to + cols_to
    for device in everyone:
        pl.semaphore_signal(barrier, inc=1, device_id=device, device_id_type=MESH)

    factor = [
        [
            scale_ref[a, b] * occupancy_ref[a, b].astype(F32)
            for b in range(cols_here // TILE)
        ]
        for a in range(rows_here // TILE)
    ]

    def fold(array):
        return jnp.max(array.reshape(LANE // 8, 8, LANE), axis=0)

    for ref in (col_peak, row_peak):
        ref[...] = jnp.zeros_like(ref)
    loads[0].wait()
    col_best = [None] * col_blocks
    for q in range(row_blocks):
        across = None
        for l in range(col_blocks):
            entries = jnp.abs(values[block(q), block(l)].astype(F32)) * factor[q // per_tile][l // per_tile]
            magnitude[block(q), block(l)] = entries
            across = entries if across is None else jnp.maximum(across, entries)
            best = fold(entries)
            col_best[l] = best if q == 0 else jnp.maximum(col_best[l], best)
        row_peak[0, q : q + 1, :] = jnp.max(across.T, axis=0, keepdims=True)
    for l in range(col_blocks):
        col_peak[0, l : l + 1, :] = jnp.max(col_best[l], axis=0, keepdims=True)

    pl.semaphore_wait(barrier, len(everyone))
    plane_base = spread(col_peak.at[0], col_first.at[0], plane_to)
    row_base = spread(row_peak.at[0], row_first.at[0], cols_to)

    def best_of(own, slots, count):
        best = own
        for k in range(count):
            best = jnp.maximum(best, slots[k])
        return best

    collect(col_first.at[0], plane_base, plane_to)
    col_peak[1] = best_of(col_peak[0], col_first.at[0], len(plane_to))
    z_base = spread(col_peak.at[1], col_second.at[0], z_to)

    collect(row_first.at[0], row_base, cols_to)
    row_scale[0] = 1.0 / jnp.sqrt(best_of(row_peak[0], row_first.at[0], len(cols_to)) + EPS)

    for q in range(row_blocks):
        down = jnp.broadcast_to(row_scale[0, q : q + 1, :], (LANE, LANE)).T
        for l in range(col_blocks):
            best = fold(magnitude[block(q), block(l)] * down)
            col_best[l] = best if q == 0 else jnp.maximum(col_best[l], best)
    for l in range(col_blocks):
        col_peak[2, l : l + 1, :] = jnp.max(col_best[l], axis=0, keepdims=True)
    plane_base = spread(col_peak.at[2], col_first.at[1], plane_to)

    collect(col_second.at[0], z_base, z_to)
    col_scale[0] = 1.0 / jnp.sqrt(best_of(col_peak[1], col_second.at[0], len(z_to)) + EPS)

    for q in range(row_blocks):
        across = None
        for l in range(col_blocks):
            entries = magnitude[block(q), block(l)] * col_scale[0, l : l + 1, :]
            across = entries if across is None else jnp.maximum(across, entries)
        row_peak[1, q : q + 1, :] = jnp.max(across.T, axis=0, keepdims=True)
    row_base = spread(row_peak.at[1], row_first.at[1], cols_to)

    collect(col_first.at[1], plane_base, plane_to)
    col_peak[3] = best_of(col_peak[2], col_first.at[1], len(plane_to))
    z_base = spread(col_peak.at[3], col_second.at[1], z_to)

    loads[1].wait()
    collect(row_first.at[1], row_base, cols_to)
    peak = best_of(row_peak[1], row_first.at[1], len(cols_to))
    row_scale[1] = row_scale[0] / jnp.sqrt(row_scale[0] * peak + EPS)

    own_half = pl.ds(pl.multiple_of(core * half_rows, half_rows), half_rows)
    other_half = pl.ds(pl.multiple_of((1 - core) * half_rows, half_rows), half_rows)

    def group_of(core_at, y_at):
        start = (core_at * Y_SIZE + y_at) * group_rows
        return pl.ds(pl.multiple_of(start, group_rows), group_rows)

    def in_half(y_at):
        return pl.ds(pl.multiple_of(y_at * group_rows, group_rows), group_rows)

    def backward(duals, step):
        scaled = [
            jnp.concatenate(
                [
                    duals[:, block(q)] * row_scale[1, q : q + 1, :]
                    for q in range(a * per_tile, (a + 1) * per_tile)
                ],
                axis=1,
            ).astype(BF16)
            for a in range(rows_here // TILE)
        ]
        for b in range(cols_here // TILE):
            at_b = slice(b * TILE, (b + 1) * TILE)
            total = None
            for a in range(rows_here // TILE):
                term = factor[a][b] * jnp.dot(
                    scaled[a],
                    values[a * TILE : (a + 1) * TILE, at_b],
                    preferred_element_type=F32,
                )
                total = term if total is None else total + term
            part[step, :, at_b] = total
        base = reserve(1)
        put(part.at[step, other_half, :], half_in.at[step], base, partner)
        return base

    def over_y(step, base):
        arrived(half_in.at[step], base, partner)
        half[step] = part[step, own_half, :] + half_in[step]
        base = reserve(len(y_offsets))
        for k, offset in enumerate(y_offsets):
            to = shift(y, offset, Y_SIZE)
            put(half.at[step, in_half(to), :], group_in.at[step, k], base + k, y_to[k])
        return base

    def over_z(step, base):
        for k, device in enumerate(y_to):
            arrived(group_in.at[step, k], base + k, device)
        total = half[step, in_half(y), :]
        for k in range(len(y_to)):
            total = total + group_in[step, k]
        high_slots[step, z_high] = total
        base = reserve(len(z_to))
        for k, device in enumerate(z_to):
            put(high_slots.at[step, z_high], high_slots.at[step, z_high], base + k, device)
        return base

    def z_slots_in(slots, base):
        for k, offset in enumerate(z_offsets):
            arrived(slots.at[shift(z_high, -offset, Z_HIGH)], base + k, z_to[k])
        total = slots[0]
        for k in range(1, Z_HIGH):
            total = total + slots[k]
        return total

    own_rows = pl.ds(pl.multiple_of(x * chunk_rows, chunk_rows), chunk_rows)
    own_cols = pl.ds(pl.multiple_of(z_low * chunk_cols, chunk_cols), chunk_cols)

    def forward(vectors, step):
        scaled = [
            jnp.concatenate(
                [
                    vectors[:, block(l)] * col_scale[1, l : l + 1, :]
                    for l in range(b * per_tile, (b + 1) * per_tile)
                ],
                axis=1,
            ).astype(BF16)
            for b in range(cols_here // TILE)
        ]
        for a in range(rows_here // TILE):
            at_a = slice(a * TILE, (a + 1) * TILE)
            total = None
            for b in range(cols_here // TILE):
                term = factor[a][b] * lax.dot_general(
                    scaled[b],
                    values[at_a, b * TILE : (b + 1) * TILE],
                    (((1,), (1,)), ((), ())),
                    preferred_element_type=F32,
                )
                total = term if total is None else total + term
            image[step, :, at_a] = total

    def over_cols(step):
        base = reserve(len(cols_to))
        for k, offset in enumerate(col_offsets):
            x_at, low_at = cols_at(offset, 1)
            rows = pl.ds(pl.multiple_of(x_at * chunk_rows, chunk_rows), chunk_rows)
            cols = pl.ds(pl.multiple_of(low_at * chunk_cols, chunk_cols), chunk_cols)
            put(image.at[step, rows, cols], image_in.at[step, k], base + k, cols_to[k])
        return base

    def image_sum(step, base):
        for k, device in enumerate(cols_to):
            arrived(image_in.at[step, k], base + k, device)
        total = image[step, own_rows, own_cols]
        for k in range(len(cols_to)):
            total = total + image_in[step, k]
        return total

    half_base = backward(y_start, 0)
    collect(col_second.at[1], z_base, z_to)
    peak = best_of(col_peak[3], col_second.at[1], len(z_to))
    col_scale[1] = col_scale[0] / jnp.sqrt(col_scale[0] * peak + EPS)
    group_base = over_y(0, half_base)
    loads[2].wait()
    forward(x_start, 0)
    first_base = over_cols(0)
    z_base = over_z(0, group_base)
    loads[3].wait()
    loads[4].wait()

    own_group = group_of(core, y)
    primal_step, dual_step = step_ref[0], step_ref[1]

    def of_block(l):
        scale = col_scale[1, l : l + 1, :]
        return (
            x_start[own_group, block(l)],
            cost[own_group, block(l)] * scale,
            low_ref[0:1, block(l)] / scale,
            high_ref[0:1, block(l)] / scale,
        )

    summed = z_slots_in(high_slots.at[0], z_base)
    for l in range(col_blocks):
        old, cost_scaled, low_scaled, high_scaled = of_block(l)
        dual = col_scale[1, l : l + 1, :] * summed[:, block(l)]
        dual_first[:, block(l)] = dual
        new = old - primal_step * (cost_scaled - dual)
        x_full[own_group, block(l)] = jnp.minimum(jnp.maximum(new, low_scaled), high_scaled)

    y_base = reserve(len(y_to))
    relay_base = reserve(Y_SIZE)
    for k, device in enumerate(y_to):
        put(x_full.at[own_group, :], x_full.at[own_group, :], y_base + k, device)
    put(x_full.at[own_group, :], x_full.at[own_group, :], relay_base + Y_SIZE - 1, partner)

    image_first[...] = image_sum(0, first_base)

    for k in reversed(range(len(y_to))):
        rows = group_of(core, shift(y, -y_offsets[k], Y_SIZE))
        arrived(x_full.at[rows, :], y_base + k, y_to[k])
        put(x_full.at[rows, :], x_full.at[rows, :], relay_base + k, partner)
    for k, offset in enumerate(y_offsets + [0]):
        rows = group_of(1 - core, shift(y, -offset, Y_SIZE))
        arrived(x_full.at[rows, :], relay_base + k, partner)

    forward(x_full, 1)
    second_base = over_cols(1)
    x_written = pltpu.make_async_copy(x_full, x_out, local.at[5])
    x_written.start()

    scale = jnp.concatenate(
        [row_scale[1, pl.ds(z_low * (chunk_cols // LANE) + j, 1), :] for j in range(chunk_cols // LANE)],
        axis=1,
    )
    y_old = y_start[own_rows, own_cols]
    rhs_scaled = rhs[own_rows, own_cols] * scale
    inequality = kind_ref[0:1, own_cols] == 1
    first = scale * image_first[...]
    second = scale * image_sum(1, second_base)
    trial = y_old + dual_step * (rhs_scaled - (2.0 * second - first))
    y_new = jnp.where(inequality, jnp.maximum(trial, 0.0), trial)
    y_full[own_rows, own_cols] = y_new
    y_base = reserve(len(cols_to))
    for k, device in enumerate(cols_to):
        put(y_full.at[own_rows, own_cols], y_full.at[own_rows, own_cols], y_base + k, device)

    def on_lanes(terms, first_row):
        sums = jnp.sum(terms, axis=1, keepdims=True)
        shape = (terms.shape[0], scenarios)
        lanes = lax.broadcasted_iota(jnp.int32, shape, 1)
        rows = lax.broadcasted_iota(jnp.int32, shape, 0)
        spread_out = jnp.where(lanes == rows + first_row, jnp.broadcast_to(sums, shape), 0.0)
        return jnp.sum(spread_out, axis=0, keepdims=True)

    violation = rhs_scaled - 0.5 * (first + second)
    violation = jnp.where(inequality, jnp.maximum(violation, 0.0), violation)
    y_mean = 0.5 * (y_old + y_new)
    y_sums[z_high] = jnp.zeros(y_sums.shape[1:], F32)
    first_row = x * chunk_rows
    y_sums[z_high, 0:1, :] = on_lanes(violation * violation, first_row)
    y_sums[z_high, 1:2, :] = on_lanes(rhs_scaled * y_mean, first_row)
    y_sums[z_high, 2:3, :] = on_lanes((y_new - y_old) * (y_new - y_old), first_row)
    sums_base = reserve(len(z_to))
    for k, device in enumerate(z_to):
        put(y_sums.at[z_high], y_sums.at[z_high], sums_base + k, device)

    for k, offset in enumerate(col_offsets):
        x_at, low_at = cols_at(offset, -1)
        rows = pl.ds(pl.multiple_of(x_at * chunk_rows, chunk_rows), chunk_rows)
        cols = pl.ds(pl.multiple_of(low_at * chunk_cols, chunk_cols), chunk_cols)
        arrived(y_full.at[rows, cols], y_base + k, cols_to[k])

    half_base = backward(y_full, 1)
    y_written = pltpu.make_async_copy(y_full, y_out, local.at[6])
    y_written.start()
    group_base = over_y(1, half_base)
    first_row = group * group_rows
    products = moves = None
    for l in range(col_blocks):
        old, cost_scaled, _, _ = of_block(l)
        new = x_full[own_group, block(l)]
        product = cost_scaled * (0.5 * (old + new))
        move = (new - old) * (new - old)
        products = product if products is None else products + product
        moves = move if moves is None else moves + move
    products, moves = on_lanes(products, first_row), on_lanes(moves, first_row)
    z_base = over_z(1, group_base)
    rows_sum = z_slots_in(y_sums, sums_base)
    summed = z_slots_in(high_slots.at[1], z_base)
    bounds = None
    for l in range(col_blocks):
        _, cost_scaled, low_scaled, high_scaled = of_block(l)
        dual = col_scale[1, l : l + 1, :] * summed[:, block(l)]
        reduced = cost_scaled - 0.5 * (dual_first[:, block(l)] + dual)
        bound = low_scaled * jnp.maximum(reduced, 0.0) - high_scaled * jnp.maximum(-reduced, 0.0)
        bounds = bound if bounds is None else bounds + bound
    sums_cols[column] = rows_sum
    sums_cols[column, 3:4, :] = products
    sums_cols[column, 4:5, :] = on_lanes(bounds, first_row)
    sums_cols[column, 5:6, :] = moves

    base = reserve(len(cols_to))
    for k, device in enumerate(cols_to):
        put(sums_cols.at[column], sums_cols.at[column], base + k, device)
    for k, offset in enumerate(col_offsets):
        x_at, low_at = cols_at(offset, -1)
        arrived(sums_cols.at[x_at * Z_LOW + low_at], base + k, cols_to[k])
    total = sums_cols[0]
    for k in range(1, X_SIZE * Z_LOW):
        total = total + sums_cols[k]
    sums_rows[group] = total
    base = reserve(len(plane_to))
    for k, device in enumerate(plane_to):
        put(sums_rows.at[group], sums_rows.at[group], base + k, device)
    for k, offset in enumerate(plane_offsets):
        y_at, core_at = plane_at(offset, -1)
        arrived(sums_rows.at[core_at * Y_SIZE + y_at], base + k, plane_to[k])
    total = sums_rows[0]
    for k in range(1, CORES * Y_SIZE):
        total = total + sums_rows[k]

    measures_ref[0:1, :] = total[0:1, :] / rows_total
    measures_ref[1:2, :] = (total[3:4, :] - total[1:2, :] - total[4:5, :]) / cols_total
    measures_ref[2:3, :] = total[2:3, :] / rows_total
    move_ref[...] = total[5:6, :] / cols_total
    x_written.wait()
    y_written.wait()
    for moved in started:
        moved.wait_send()


def per_device(
    values,
    tile_scale,
    occupancy,
    row_kind,
    right_side,
    cost_vector,
    lower_bound,
    upper_bound,
    x_start,
    y_start,
    step_sizes,
):
    rows_here, cols_here = values.shape
    scenarios = x_start.shape[0]
    plane, cols_size = CORES * Y_SIZE, X_SIZE * Z_LOW
    group_rows, half_rows = scenarios // plane, scenarios // CORES
    chunk = (scenarios // X_SIZE, rows_here // Z_LOW)
    semaphores = 2 * (plane + Z_HIGH + cols_size - 3) + 2 * (1 + Y_SIZE + Z_HIGH - 2)
    semaphores += 2 * Y_SIZE - 1 + 3 * (cols_size - 1) + Z_HIGH - 1 + cols_size - 1 + plane - 1
    vmem, smem, anywhere = (
        pl.BlockSpec(memory_space=space) for space in (pltpu.VMEM, pltpu.SMEM, pl.ANY)
    )
    x_next, y_next, measures, move = pl.pallas_call(
        kernel,
        out_shape=(
            jax.ShapeDtypeStruct((scenarios, cols_here), F32),
            jax.ShapeDtypeStruct((scenarios, rows_here), F32),
            jax.ShapeDtypeStruct((3, scenarios), F32),
            jax.ShapeDtypeStruct((1, scenarios), F32),
        ),
        in_specs=[
            anywhere,
            smem,
            smem,
            vmem,
            anywhere,
            anywhere,
            vmem,
            vmem,
            anywhere,
            anywhere,
            smem,
        ],
        out_specs=(anywhere, anywhere, vmem, vmem),
        scratch_shapes=[
            pltpu.VMEM((rows_here, cols_here), BF16),
            pltpu.VMEM((scenarios, rows_here), F32),
            pltpu.VMEM((scenarios, cols_here), F32),
            pltpu.VMEM((scenarios, cols_here), F32),
            pltpu.VMEM((scenarios, rows_here), F32),
            pltpu.VMEM((rows_here, cols_here), F32),
            pltpu.VMEM((4, 8, LANE), F32),
            pltpu.VMEM((2, 8, LANE), F32),
            pltpu.VMEM((2, plane - 1, 8, LANE), F32),
            pltpu.VMEM((2, cols_size - 1, 8, LANE), F32),
            pltpu.VMEM((2, Z_HIGH - 1, 8, LANE), F32),
            pltpu.VMEM((2, 8, LANE), F32),
            pltpu.VMEM((2, 8, LANE), F32),
            pltpu.VMEM((2, scenarios, cols_here), F32),
            pltpu.VMEM((2, half_rows, cols_here), F32),
            pltpu.VMEM((2, half_rows, cols_here), F32),
            pltpu.VMEM((2, Y_SIZE - 1, group_rows, cols_here), F32),
            pltpu.VMEM((2, Z_HIGH, group_rows, cols_here), F32),
            pltpu.VMEM((group_rows, cols_here), F32),
            pltpu.VMEM((scenarios, cols_here), F32),
            pltpu.VMEM((2, scenarios, rows_here), F32),
            pltpu.VMEM((2, cols_size - 1) + chunk, F32),
            pltpu.VMEM(chunk, F32),
            pltpu.VMEM((scenarios, rows_here), F32),
            pltpu.VMEM((Z_HIGH, 8, scenarios), F32),
            pltpu.VMEM((cols_size, 8, scenarios), F32),
            pltpu.VMEM((plane, 8, scenarios), F32),
            pltpu.SemaphoreType.DMA((semaphores,)),
            pltpu.SemaphoreType.DMA((semaphores,)),
            pltpu.SemaphoreType.DMA((7,)),
        ],
        compiler_params=pltpu.CompilerParams(
            collective_id=0, has_side_effects=True, vmem_limit_bytes=32 << 20
        ),
    )(
        values,
        tile_scale,
        occupancy,
        row_kind.reshape(1, -1),
        right_side,
        cost_vector,
        lower_bound.reshape(1, -1),
        upper_bound.reshape(1, -1),
        x_start,
        y_start,
        step_sizes,
    )
    return x_next, y_next, measures, move.reshape(-1)


def solution(mesh):
    return jax.shard_map(
        per_device,
        mesh=mesh,
        in_specs=(
            P("rows", "cols"),
            P("rows", "cols"),
            P("rows", "cols"),
            P("rows"),
            P(None, "rows"),
            P(None, "cols"),
            P("cols"),
            P("cols"),
            P(None, "cols"),
            P(None, "rows"),
            P(),
        ),
        out_specs=(P(None, "cols"), P(None, "rows"), P(), P()),
        check_vma=False,
    )
```

time: 1580 us -> 108 us (0.07)
  waiting for transfers between devices: 973 us -> 0 us
  blocking collectives: 558 us -> 0 us
  Pallas kernels: 0 us -> 97.5 us
    psum x3 -> x0, waiting for transfers between devices: 972 us -> none  [the longest x2 845 us: dual_image(): return lax.psum(partial_value, 'rows')]
    pmax x4 -> x0, blocking collectives: 373 us -> none  [the longest x2 324 us: per_device(): col_peak = lax.pmax(col_peak, 'rows')]
    psum x2 -> x0, blocking collectives: 185 us -> none  [the longest x1 161 us: per_device(): y_total = lax.psum(y_terms, 'rows')]
    pallas_call x0 -> x1, Pallas kernels: none -> 97.5 us  [per_device(): pl.pallas_call(kernel, out_shape=(jax.ShapeDtypeStruct((scenarios, cols_h...]
  transfers between devices with their start and end apart: 3 -> 0, of which waited for: 3 -> 0; matrix products, arithmetic and copies ran while one was open for 0% -> 0% of each run, Pallas kernels for 0% -> 0%
where the time goes in v1:
time: 108 us; the launch traced here: 107 us
  Pallas kernels  97.5 us (90%)
  local copies, waits for them, and re-layouts  9.09 us (8%)
    pallas_call x1, Pallas kernels, per_device(): pl.pallas_call(kernel, out_shape=(jax.ShapeDtypeStruct((scenarios, cols_h...  97.5 us
    unnamed x28, local copies, waits for them, and re-layouts  9.09 us

profile of v1, /device:TPU:1, one launch (start us, length us, event | category | flops | bytes accessed | tf_op | source)
XLA Modules:
  0.0 107.2 jit_solution(6238061351736731890)
XLA Ops:
  0.6 0.0 copy-start.9
  0.6 0.0 copy-start.10
  0.7 0.0 copy-start.8
  0.7 0.7 copy-done.9
  1.3 0.1 copy.15.scale_ref
  1.4 0.0 copy-done.10
  1.4 0.1 copy.16.occupancy_ref
  1.5 0.0 copy-done.8
  1.5 0.0 copy-start.5
  1.5 0.0 copy-start.6
  1.5 0.0 copy-start.7
  1.5 0.7 copy-done.5
  2.2 0.0 copy-done.6
  2.2 0.0 copy-done.7
  2.2 0.0 copy-start
  2.2 1.1 %copy-done = bf16[768,512]{1,0:T(8,128)(2,1)S(1)} copy-done((bf16[768,512]{1,0:T(8,128)(2,1)S(1)}, bf16[768,512]{1,0:T(8,128)(2,1)}, u32[]{:S(2)}) %copy-start) | copy-done | bytes 786456
  3.3 0.0 copy-start.1
  3.3 1.0 copy-done.1
  4.3 0.0 copy-start.2
  4.3 1.0 copy-done.2
  5.3 0.0 copy-start.3
  5.3 0.9 copy-done.3
  6.3 0.0 copy-start.4
  6.3 0.9 copy-done.4
  7.2 97.5 %shard_map.138 = (f32[128,512]{1,0:T(8,128)S(1)}, f32[128,768]{1,0:T(8,128)S(1)}, f32[3,128]{1,0:T(4,128)S(1)}, f32[1,128]{1,0:T(1,128)S(1)}) custom-call(bf16[768,512]{1,0:T(8,128)(2,1)S(1)} %copy-done, f32[3,2]{1,0:T(4,128)S(1)} %copy.15.scale_ref, s32[3,2]{1,0:T(4,128)S(1)} %copy.16.occupancy_ref, s32[1,768]{1,0:T(1,128)S(1)} %reshape.20.kind_ref, ...), custom_call_target="tpu_custom_call" | custom-call | tf_op jit(solution)/shard_map/pallas_call | solution.py:532
  104.7 0.7 copy.21
  105.4 0.7 copy.22
  106.1 0.6 copy.23
  106.7 0.5 copy.24
  (1 shorter events, 0.0 us)
Async XLA Ops:
  0.6 0.7 copy-start.9
  0.6 0.8 copy-start.10
  0.7 0.9 copy-start.8
  1.5 0.7 copy-start.5
  1.5 0.7 copy-start.6
  1.5 0.7 copy-start.7
  2.2 1.1 %copy-start = (bf16[768,512]{1,0:T(8,128)(2,1)S(1)}, bf16[768,512]{1,0:T(8,128)(2,1)}, u32[]{:S(2)}) copy-start(bf16[768,512]{1,0:T(8,128)(2,1)} %values_in.1) | copy-start | bytes 2359300
  3.3 1.0 copy-start.1
  4.3 1.0 copy-start.2
  5.3 0.9 copy-start.3
  6.3 0.9 copy-start.4

commit v2 on v1

--- a/solution.py
+++ b/solution.py
@@ -22,16 +22,16 @@
 
 def kernel(
     values_in,
-    scale_ref,
-    occupancy_ref,
-    kind_ref,
+    scale_in,
+    occupancy_in,
+    kind_in,
     rhs_in,
     cost_in,
-    low_ref,
-    high_ref,
+    low_in,
+    high_in,
     x_in,
     y_in,
-    step_ref,
+    step_in,
     x_out,
     y_out,
     measures_ref,
@@ -41,6 +41,12 @@
     cost,
     x_start,
     y_start,
+    scale_ref,
+    occupancy_ref,
+    kind_ref,
+    low_ref,
+    high_ref,
+    step_ref,
     magnitude,
     col_peak,
     row_peak,
@@ -49,7 +55,8 @@
     col_second,
     col_scale,
     row_scale,
-    part,
+    scaled_duals,
+    half_out,
     half_in,
     half,
     group_in,
@@ -60,9 +67,12 @@
     image_in,
     image_first,
     y_full,
+    bounds_scaled,
     y_sums,
-    sums_cols,
-    sums_rows,
+    early_cols,
+    early_rows,
+    late_cols,
+    late_rows,
     send,
     recv,
     local,
@@ -154,13 +164,39 @@
         for k, device in enumerate(peers):
             arrived(slots.at[k], base + k, device)
 
+    def share(slots, own, targets):
+        base = reserve(len(targets))
+        for k, device in enumerate(targets):
+            put(slots.at[own], slots.at[own], base + k, device)
+        return base
+
+    def added(slots, sources, base, targets):
+        for k, device in enumerate(targets):
+            arrived(slots.at[sources[k]], base + k, device)
+        total = slots[0]
+        for k in range(1, slots.shape[0]):
+            total = total + slots[k]
+        return total
+
     def block(index):
         return slice(index * LANE, (index + 1) * LANE)
 
     loads = [
         pltpu.make_async_copy(source, target, local.at[k])
         for k, (source, target) in enumerate(
-            [(values_in, values), (y_in, y_start), (x_in, x_start), (cost_in, cost), (rhs_in, rhs)]
+            [
+                (scale_in, scale_ref),
+                (occupancy_in, occupancy_ref),
+                (values_in, values),
+                (y_in, y_start),
+                (x_in, x_start),
+                (cost_in, cost),
+                (rhs_in, rhs),
+                (low_in, low_ref),
+                (high_in, high_ref),
+                (step_in, step_ref),
+            ]
+            + [(kind_in.at[block(q)], kind_ref.at[q]) for q in range(row_blocks)]
         )
     ]
     for load in loads:
@@ -169,10 +205,12 @@
     everyone = plane_to + z_to + cols_to
     for device in everyone:
         pl.semaphore_signal(barrier, inc=1, device_id=device, device_id_type=MESH)
+    loads[0].wait()
+    loads[1].wait()
 
     factor = [
         [
-            scale_ref[a, b] * occupancy_ref[a, b].astype(F32)
+            scale_ref[b, a] * occupancy_ref[b, a].astype(F32)
             for b in range(cols_here // TILE)
         ]
         for a in range(rows_here // TILE)
@@ -181,9 +219,7 @@
     def fold(array):
         return jnp.max(array.reshape(LANE // 8, 8, LANE), axis=0)
 
-    for ref in (col_peak, row_peak):
-        ref[...] = jnp.zeros_like(ref)
-    loads[0].wait()
+    loads[2].wait()
     col_best = [None] * col_blocks
     for q in range(row_blocks):
         across = None
@@ -238,7 +274,7 @@
     col_peak[3] = best_of(col_peak[2], col_first.at[1], len(plane_to))
     z_base = spread(col_peak.at[3], col_second.at[1], z_to)
 
-    loads[1].wait()
+    loads[3].wait()
     collect(row_first.at[1], row_base, cols_to)
     peak = best_of(row_peak[1], row_first.at[1], len(cols_to))
     row_scale[1] = row_scale[0] / jnp.sqrt(row_scale[0] * peak + EPS)
@@ -264,24 +300,30 @@
             ).astype(BF16)
             for a in range(rows_here // TILE)
         ]
-        for b in range(cols_here // TILE):
-            at_b = slice(b * TILE, (b + 1) * TILE)
-            total = None
-            for a in range(rows_here // TILE):
-                term = factor[a][b] * jnp.dot(
-                    scaled[a],
-                    values[a * TILE : (a + 1) * TILE, at_b],
-                    preferred_element_type=F32,
-                )
-                total = term if total is None else total + term
-            part[step, :, at_b] = total
+        for a in range(rows_here // TILE):
+            scaled_duals[:, a * TILE : (a + 1) * TILE] = scaled[a]
+
+        def product(rows, target):
+            for b in range(cols_here // TILE):
+                at_b = slice(b * TILE, (b + 1) * TILE)
+                total = None
+                for a in range(rows_here // TILE):
+                    at_a = slice(a * TILE, (a + 1) * TILE)
+                    term = factor[a][b] * jnp.dot(
+                        scaled_duals[rows, at_a], values[at_a, at_b], preferred_element_type=F32
+                    )
+                    total = term if total is None else total + term
+                target[step, :, at_b] = total
+
+        product(other_half, half_out)
         base = reserve(1)
-        put(part.at[step, other_half, :], half_in.at[step], base, partner)
+        put(half_out.at[step], half_in.at[step], base, partner)
+        product(own_half, half)
         return base
 
     def over_y(step, base):
         arrived(half_in.at[step], base, partner)
-        half[step] = part[step, own_half, :] + half_in[step]
+        half[step] = half[step] + half_in[step]
         base = reserve(len(y_offsets))
         for k, offset in enumerate(y_offsets):
             to = shift(y, offset, Y_SIZE)
@@ -309,7 +351,7 @@
         return total
 
     own_rows = pl.ds(pl.multiple_of(x * chunk_rows, chunk_rows), chunk_rows)
-    own_cols = pl.ds(pl.multiple_of(z_low * chunk_cols, chunk_cols), chunk_cols)
+    pieces = chunk_cols // LANE
 
     def forward(vectors, step):
         scaled = [
@@ -335,21 +377,27 @@
                 total = term if total is None else total + term
             image[step, :, at_a] = total
 
-    def over_cols(step):
+    def rows_of(x_at):
+        return pl.ds(pl.multiple_of(x_at * chunk_rows, chunk_rows), chunk_rows)
+
+    def lanes_of(low_at, piece):
+        start = low_at * chunk_cols + piece * LANE
+        return pl.ds(pl.multiple_of(start, LANE), LANE)
+
+    def over_cols(step, piece):
         base = reserve(len(cols_to))
         for k, offset in enumerate(col_offsets):
             x_at, low_at = cols_at(offset, 1)
-            rows = pl.ds(pl.multiple_of(x_at * chunk_rows, chunk_rows), chunk_rows)
-            cols = pl.ds(pl.multiple_of(low_at * chunk_cols, chunk_cols), chunk_cols)
-            put(image.at[step, rows, cols], image_in.at[step, k], base + k, cols_to[k])
+            source = image.at[step, rows_of(x_at), lanes_of(low_at, piece)]
+            put(source, image_in.at[step, piece, k], base + k, cols_to[k])
         return base
 
-    def image_sum(step, base):
+    def image_sum(step, piece, base):
         for k, device in enumerate(cols_to):
-            arrived(image_in.at[step, k], base + k, device)
-        total = image[step, own_rows, own_cols]
+            arrived(image_in.at[step, piece, k], base + k, device)
+        total = image[step, own_rows, lanes_of(z_low, piece)]
         for k in range(len(cols_to)):
-            total = total + image_in[step, k]
+            total = total + image_in[step, piece, k]
         return total
 
     half_base = backward(y_start, 0)
@@ -357,28 +405,27 @@
     peak = best_of(col_peak[3], col_second.at[1], len(z_to))
     col_scale[1] = col_scale[0] / jnp.sqrt(col_scale[0] * peak + EPS)
     group_base = over_y(0, half_base)
-    loads[2].wait()
+    loads[4].wait()
     forward(x_start, 0)
-    first_base = over_cols(0)
     z_base = over_z(0, group_base)
-    loads[3].wait()
-    loads[4].wait()
+    first_bases = [over_cols(0, piece) for piece in range(pieces)]
+    for load in loads[5:]:
+        load.wait()
 
     own_group = group_of(core, y)
     primal_step, dual_step = step_ref[0], step_ref[1]
 
-    def of_block(l):
-        scale = col_scale[1, l : l + 1, :]
-        return (
-            x_start[own_group, block(l)],
-            cost[own_group, block(l)] * scale,
-            low_ref[0:1, block(l)] / scale,
-            high_ref[0:1, block(l)] / scale,
-        )
+    for l in range(col_blocks):
+        col = col_scale[1, l : l + 1, :]
+        wide = (group_rows, LANE)
+        bounds_scaled[0, :, block(l)] = cost[own_group, block(l)] * col
+        bounds_scaled[1, :, block(l)] = jnp.broadcast_to(low_ref[0:1, block(l)] / col, wide)
+        bounds_scaled[2, :, block(l)] = jnp.broadcast_to(high_ref[0:1, block(l)] / col, wide)
 
     summed = z_slots_in(high_slots.at[0], z_base)
     for l in range(col_blocks):
-        old, cost_scaled, low_scaled, high_scaled = of_block(l)
+        old = x_start[own_group, block(l)]
+        cost_scaled, low_scaled, high_scaled = (bounds_scaled[k, :, block(l)] for k in range(3))
         dual = col_scale[1, l : l + 1, :] * summed[:, block(l)]
         dual_first[:, block(l)] = dual
         new = old - primal_step * (cost_scaled - dual)
@@ -390,7 +437,8 @@
         put(x_full.at[own_group, :], x_full.at[own_group, :], y_base + k, device)
     put(x_full.at[own_group, :], x_full.at[own_group, :], relay_base + Y_SIZE - 1, partner)
 
-    image_first[...] = image_sum(0, first_base)
+    for piece in range(pieces):
+        image_first[:, block(piece)] = image_sum(0, piece, first_bases[piece])
 
     for k in reversed(range(len(y_to))):
         rows = group_of(core, shift(y, -y_offsets[k], Y_SIZE))
@@ -401,25 +449,37 @@
         arrived(x_full.at[rows, :], relay_base + k, partner)
 
     forward(x_full, 1)
-    second_base = over_cols(1)
-    x_written = pltpu.make_async_copy(x_full, x_out, local.at[5])
+    second_bases = [over_cols(1, piece) for piece in range(pieces)]
+    x_written = pltpu.make_async_copy(x_full, x_out, local.at[len(loads)])
     x_written.start()
 
-    scale = jnp.concatenate(
-        [row_scale[1, pl.ds(z_low * (chunk_cols // LANE) + j, 1), :] for j in range(chunk_cols // LANE)],
-        axis=1,
-    )
-    y_old = y_start[own_rows, own_cols]
-    rhs_scaled = rhs[own_rows, own_cols] * scale
-    inequality = kind_ref[0:1, own_cols] == 1
-    first = scale * image_first[...]
-    second = scale * image_sum(1, second_base)
-    trial = y_old + dual_step * (rhs_scaled - (2.0 * second - first))
-    y_new = jnp.where(inequality, jnp.maximum(trial, 0.0), trial)
-    y_full[own_rows, own_cols] = y_new
-    y_base = reserve(len(cols_to))
-    for k, device in enumerate(cols_to):
-        put(y_full.at[own_rows, own_cols], y_full.at[own_rows, own_cols], y_base + k, device)
+    y_bases = []
+    violations = products = moves = None
+
+    def add(total, term):
+        return term if total is None else total + term
+
+    for piece in range(pieces):
+        lanes = lanes_of(z_low, piece)
+        line = pl.ds(z_low * pieces + piece, 1)
+        scale = row_scale[1, line, :]
+        y_old = y_start[own_rows, lanes]
+        rhs_scaled = rhs[own_rows, lanes] * scale
+        inequality = kind_ref[line, :] == 1
+        first = scale * image_first[:, block(piece)]
+        second = scale * image_sum(1, piece, second_bases[piece])
+        trial = y_old + dual_step * (rhs_scaled - (2.0 * second - first))
+        y_new = jnp.where(inequality, jnp.maximum(trial, 0.0), trial)
+        y_full[own_rows, lanes] = y_new
+        base = reserve(len(cols_to))
+        for k, device in enumerate(cols_to):
+            put(y_full.at[own_rows, lanes], y_full.at[own_rows, lanes], base + k, device)
+        y_bases.append(base)
+        violation = rhs_scaled - 0.5 * (first + second)
+        violation = jnp.where(inequality, jnp.maximum(violation, 0.0), violation)
+        violations = add(violations, violation * violation)
+        products = add(products, rhs_scaled * (0.5 * (y_old + y_new)))
+        moves = add(moves, (y_new - y_old) * (y_new - y_old))
 
     def on_lanes(terms, first_row):
         sums = jnp.sum(terms, axis=1, keepdims=True)
@@ -429,81 +489,71 @@
         spread_out = jnp.where(lanes == rows + first_row, jnp.broadcast_to(sums, shape), 0.0)
         return jnp.sum(spread_out, axis=0, keepdims=True)
 
-    violation = rhs_scaled - 0.5 * (first + second)
-    violation = jnp.where(inequality, jnp.maximum(violation, 0.0), violation)
-    y_mean = 0.5 * (y_old + y_new)
-    y_sums[z_high] = jnp.zeros(y_sums.shape[1:], F32)
     first_row = x * chunk_rows
-    y_sums[z_high, 0:1, :] = on_lanes(violation * violation, first_row)
-    y_sums[z_high, 1:2, :] = on_lanes(rhs_scaled * y_mean, first_row)
-    y_sums[z_high, 2:3, :] = on_lanes((y_new - y_old) * (y_new - y_old), first_row)
-    sums_base = reserve(len(z_to))
-    for k, device in enumerate(z_to):
-        put(y_sums.at[z_high], y_sums.at[z_high], sums_base + k, device)
-
-    for k, offset in enumerate(col_offsets):
-        x_at, low_at = cols_at(offset, -1)
-        rows = pl.ds(pl.multiple_of(x_at * chunk_rows, chunk_rows), chunk_rows)
-        cols = pl.ds(pl.multiple_of(low_at * chunk_cols, chunk_cols), chunk_cols)
-        arrived(y_full.at[rows, cols], y_base + k, cols_to[k])
+    y_sums[z_high, 0:1, :] = on_lanes(violations, first_row)
+    y_sums[z_high, 1:2, :] = on_lanes(products, first_row)
+    y_sums[z_high, 2:3, :] = on_lanes(moves, first_row)
+    sums_base = share(y_sums, z_high, z_to)
+
+    for piece in range(pieces):
+        for k, offset in enumerate(col_offsets):
+            x_at, low_at = cols_at(offset, -1)
+            target = y_full.at[rows_of(x_at), lanes_of(low_at, piece)]
+            arrived(target, y_bases[piece] + k, cols_to[k])
 
     half_base = backward(y_full, 1)
-    y_written = pltpu.make_async_copy(y_full, y_out, local.at[6])
+    y_written = pltpu.make_async_copy(y_full, y_out, local.at[len(loads) + 1])
     y_written.start()
     group_base = over_y(1, half_base)
     first_row = group * group_rows
     products = moves = None
     for l in range(col_blocks):
-        old, cost_scaled, _, _ = of_block(l)
-        new = x_full[own_group, block(l)]
-        product = cost_scaled * (0.5 * (old + new))
-        move = (new - old) * (new - old)
-        products = product if products is None else products + product
-        moves = move if moves is None else moves + move
-    products, moves = on_lanes(products, first_row), on_lanes(moves, first_row)
+        old, new = x_start[own_group, block(l)], x_full[own_group, block(l)]
+        products = add(products, bounds_scaled[0, :, block(l)] * (0.5 * (old + new)))
+        moves = add(moves, (new - old) * (new - old))
+    z_from = [shift(z_high, -k, Z_HIGH) for k in z_offsets]
+    cols_from = [cols_at(o, -1)[0] * Z_LOW + cols_at(o, -1)[1] for o in col_offsets]
+    plane_from = [plane_at(o, -1)[1] * Y_SIZE + plane_at(o, -1)[0] for o in plane_offsets]
+    early_cols[column, 3:4, :] = on_lanes(products, first_row)
+    early_cols[column, 4:5, :] = on_lanes(moves, first_row)
+    early_cols[column, 0:3, :] = added(y_sums, z_from, sums_base, z_to)
+    early_base = share(early_cols, column, cols_to)
     z_base = over_z(1, group_base)
-    rows_sum = z_slots_in(y_sums, sums_base)
+    early_rows[group] = added(early_cols, cols_from, early_base, cols_to)
+    early_base = share(early_rows, group, plane_to)
     summed = z_slots_in(high_slots.at[1], z_base)
     bounds = None
     for l in range(col_blocks):
-        _, cost_scaled, low_scaled, high_scaled = of_block(l)
+        cost_scaled, low_scaled, high_scaled = (bounds_scaled[k, :, block(l)] for k in range(3))
         dual = col_scale[1, l : l + 1, :] * summed[:, block(l)]
         reduced = cost_scaled - 0.5 * (dual_first[:, block(l)] + dual)
         bound = low_scaled * jnp.maximum(reduced, 0.0) - high_scaled * jnp.maximum(-reduced, 0.0)
         bounds = bound if bounds is None else bounds + bound
-    sums_cols[column] = rows_sum
-    sums_cols[column, 3:4, :] = products
-    sums_cols[column, 4:5, :] = on_lanes(bounds, first_row)
-    sums_cols[column, 5:6, :] = moves
-
-    base = reserve(len(cols_to))
-    for k, device in enumerate(cols_to):
-        put(sums_cols.at[column], sums_cols.at[column], base + k, device)
-    for k, offset in enumerate(col_offsets):
-        x_at, low_at = cols_at(offset, -1)
-        arrived(sums_cols.at[x_at * Z_LOW + low_at], base + k, cols_to[k])
-    total = sums_cols[0]
-    for k in range(1, X_SIZE * Z_LOW):
-        total = total + sums_cols[k]
-    sums_rows[group] = total
-    base = reserve(len(plane_to))
-    for k, device in enumerate(plane_to):
-        put(sums_rows.at[group], sums_rows.at[group], base + k, device)
-    for k, offset in enumerate(plane_offsets):
-        y_at, core_at = plane_at(offset, -1)
-        arrived(sums_rows.at[core_at * Y_SIZE + y_at], base + k, plane_to[k])
-    total = sums_rows[0]
-    for k in range(1, CORES * Y_SIZE):
-        total = total + sums_rows[k]
-
+    late_cols[column] = on_lanes(bounds, first_row)
+    base = share(late_cols, column, cols_to)
+    late_rows[group] = added(late_cols, cols_from, base, cols_to)
+    base = share(late_rows, group, plane_to)
+    total = added(early_rows, plane_from, early_base, plane_to)
     measures_ref[0:1, :] = total[0:1, :] / rows_total
-    measures_ref[1:2, :] = (total[3:4, :] - total[1:2, :] - total[4:5, :]) / cols_total
     measures_ref[2:3, :] = total[2:3, :] / rows_total
-    move_ref[...] = total[5:6, :] / cols_total
+    move_ref[...] = total[4:5, :] / cols_total
     x_written.wait()
     y_written.wait()
-    for moved in started:
+    for moved in started[: -len(plane_to)]:
         moved.wait_send()
+    bound_total = added(late_rows, plane_from, base, plane_to)
+    measures_ref[1:2, :] = (total[3:4, :] - total[1:2, :] - bound_total) / cols_total
+    for moved in started[-len(plane_to) :]:
+        moved.wait_send()
+
+
+def write_out(*refs):
+    sources, targets, done = refs[:4], refs[4:8], refs[8]
+    writes = [pltpu.make_async_copy(sources[k], targets[k], done.at[k]) for k in range(4)]
+    for write in writes:
+        write.start()
+    for write in writes:
+        write.wait()
 
 
 def per_device(
@@ -522,34 +572,23 @@
     rows_here, cols_here = values.shape
     scenarios = x_start.shape[0]
     plane, cols_size = CORES * Y_SIZE, X_SIZE * Z_LOW
+    row_blocks, col_blocks = rows_here // LANE, cols_here // LANE
     group_rows, half_rows = scenarios // plane, scenarios // CORES
     chunk = (scenarios // X_SIZE, rows_here // Z_LOW)
     semaphores = 2 * (plane + Z_HIGH + cols_size - 3) + 2 * (1 + Y_SIZE + Z_HIGH - 2)
-    semaphores += 2 * Y_SIZE - 1 + 3 * (cols_size - 1) + Z_HIGH - 1 + cols_size - 1 + plane - 1
-    vmem, smem, anywhere = (
-        pl.BlockSpec(memory_space=space) for space in (pltpu.VMEM, pltpu.SMEM, pl.ANY)
+    semaphores += 2 * Y_SIZE - 1 + 3 * (chunk[1] // LANE) * (cols_size - 1) + Z_HIGH - 1 + 2 * (cols_size - 1 + plane - 1)
+    vmem, hbm, anywhere = (
+        pl.BlockSpec(memory_space=space) for space in (pltpu.VMEM, pltpu.HBM, pl.ANY)
     )
     x_next, y_next, measures, move = pl.pallas_call(
         kernel,
         out_shape=(
-            jax.ShapeDtypeStruct((scenarios, cols_here), F32),
-            jax.ShapeDtypeStruct((scenarios, rows_here), F32),
-            jax.ShapeDtypeStruct((3, scenarios), F32),
-            jax.ShapeDtypeStruct((1, scenarios), F32),
+            pltpu.VMEM((scenarios, cols_here), F32),
+            pltpu.VMEM((scenarios, rows_here), F32),
+            pltpu.VMEM((3, scenarios), F32),
+            pltpu.VMEM((1, scenarios), F32),
         ),
-        in_specs=[
-            anywhere,
-            smem,
-            smem,
-            vmem,
-            anywhere,
-            anywhere,
-            vmem,
-            vmem,
-            anywhere,
-            anywhere,
-            smem,
-        ],
+        in_specs=[hbm] * 11,
         out_specs=(anywhere, anywhere, vmem, vmem),
         scratch_shapes=[
             pltpu.VMEM((rows_here, cols_here), BF16),
@@ -557,15 +596,22 @@
             pltpu.VMEM((scenarios, cols_here), F32),
             pltpu.VMEM((scenarios, cols_here), F32),
             pltpu.VMEM((scenarios, rows_here), F32),
+            pltpu.SMEM((cols_here // TILE, rows_here // TILE), F32),
+            pltpu.SMEM((cols_here // TILE, rows_here // TILE), jnp.int32),
+            pltpu.VMEM((8, LANE), jnp.int32),
+            pltpu.VMEM((1, cols_here), F32),
+            pltpu.VMEM((1, cols_here), F32),
+            pltpu.SMEM((2,), F32),
             pltpu.VMEM((rows_here, cols_here), F32),
-            pltpu.VMEM((4, 8, LANE), F32),
-            pltpu.VMEM((2, 8, LANE), F32),
-            pltpu.VMEM((2, plane - 1, 8, LANE), F32),
-            pltpu.VMEM((2, cols_size - 1, 8, LANE), F32),
-            pltpu.VMEM((2, Z_HIGH - 1, 8, LANE), F32),
-            pltpu.VMEM((2, 8, LANE), F32),
-            pltpu.VMEM((2, 8, LANE), F32),
-            pltpu.VMEM((2, scenarios, cols_here), F32),
+            pltpu.VMEM((4, col_blocks, LANE), F32),
+            pltpu.VMEM((2, row_blocks, LANE), F32),
+            pltpu.VMEM((2, plane - 1, col_blocks, LANE), F32),
+            pltpu.VMEM((2, cols_size - 1, row_blocks, LANE), F32),
+            pltpu.VMEM((2, Z_HIGH - 1, col_blocks, LANE), F32),
+            pltpu.VMEM((2, col_blocks, LANE), F32),
+            pltpu.VMEM((2, row_blocks, LANE), F32),
+            pltpu.VMEM((scenarios, rows_here), BF16),
+            pltpu.VMEM((2, half_rows, cols_here), F32),
             pltpu.VMEM((2, half_rows, cols_here), F32),
             pltpu.VMEM((2, half_rows, cols_here), F32),
             pltpu.VMEM((2, Y_SIZE - 1, group_rows, cols_here), F32),
@@ -573,32 +619,48 @@
             pltpu.VMEM((group_rows, cols_here), F32),
             pltpu.VMEM((scenarios, cols_here), F32),
             pltpu.VMEM((2, scenarios, rows_here), F32),
-            pltpu.VMEM((2, cols_size - 1) + chunk, F32),
+            pltpu.VMEM((2, chunk[1] // LANE, cols_size - 1, chunk[0], LANE), F32),
             pltpu.VMEM(chunk, F32),
             pltpu.VMEM((scenarios, rows_here), F32),
-            pltpu.VMEM((Z_HIGH, 8, scenarios), F32),
-            pltpu.VMEM((cols_size, 8, scenarios), F32),
-            pltpu.VMEM((plane, 8, scenarios), F32),
+            pltpu.VMEM((3, group_rows, cols_here), F32),
+            pltpu.VMEM((Z_HIGH, 3, scenarios), F32),
+            pltpu.VMEM((cols_size, 5, scenarios), F32),
+            pltpu.VMEM((plane, 5, scenarios), F32),
+            pltpu.VMEM((cols_size, 1, scenarios), F32),
+            pltpu.VMEM((plane, 1, scenarios), F32),
             pltpu.SemaphoreType.DMA((semaphores,)),
             pltpu.SemaphoreType.DMA((semaphores,)),
-            pltpu.SemaphoreType.DMA((7,)),
+            pltpu.SemaphoreType.DMA((12 + rows_here // LANE,)),
         ],
         compiler_params=pltpu.CompilerParams(
             collective_id=0, has_side_effects=True, vmem_limit_bytes=32 << 20
         ),
     )(
-        values,
-        tile_scale,
-        occupancy,
-        row_kind.reshape(1, -1),
-        right_side,
-        cost_vector,
-        lower_bound.reshape(1, -1),
-        upper_bound.reshape(1, -1),
-        x_start,
-        y_start,
-        step_sizes,
+        *[
+            pltpu.with_memory_space_constraint(given, pltpu.HBM)
+            for given in (
+                values,
+                tile_scale.T,
+                occupancy.T,
+                row_kind,
+                right_side,
+                cost_vector,
+                lower_bound.reshape(1, -1),
+                upper_bound.reshape(1, -1),
+                x_start,
+                y_start,
+                step_sizes,
+            )
+        ]
     )
+    results = (x_next, y_next, measures, move)
+    x_next, y_next, measures, move = pl.pallas_call(
+        write_out,
+        out_shape=tuple(pltpu.HBM(r.shape, r.dtype) for r in results),
+        in_specs=[vmem] * 4,
+        out_specs=(hbm,) * 4,
+        scratch_shapes=[pltpu.SemaphoreType.DMA((4,))],
+    )(*[pltpu.with_memory_space_constraint(r, pltpu.VMEM) for r in results])
     return x_next, y_next, measures, move.reshape(-1)
 
 

time: 108 us -> 95.9 us (0.89)
  local copies, waits for them, and re-layouts: 9.09 us -> 0 us
  Pallas kernels: 97.5 us -> 95.1 us
    unnamed x28 -> x0, local copies, waits for them, and re-layouts: 9.09 us -> none
    pallas_call x1 -> x2, Pallas kernels: 97.5 us -> 95.1 us  [the longest x1 94.2 us: per_device(): pl.pallas_call(kernel, out_shape=(pltpu.VMEM((scenarios, cols_here), F32)...]
where the time goes in v2:
time: 95.9 us; the launch traced here: 95.7 us
  Pallas kernels  95.1 us (99%)
    pallas_call x1, Pallas kernels, per_device(): pl.pallas_call(kernel, out_shape=(pltpu.VMEM((scenarios, cols_here), F32)...  94.2 us

profile of v2, /device:TPU:1, one launch (start us, length us, event | category | flops | bytes accessed | tf_op | source)
XLA Modules:
  0.0 95.7 jit_solution(7667128226505074203)
XLA Ops:
  0.6 94.2 %shard_map.138 = (f32[128,512]{1,0:T(8,128)S(1)}, f32[128,768]{1,0:T(8,128)S(1)}, f32[3,128]{1,0:T(4,128)S(1)}, f32[1,128]{1,0:T(1,128)S(1)}) custom-call(bf16[768,512]{1,0:T(8,128)(2,1)} %values_in.1, f32[2,3]{1,0:T(2,128)} %bitcast.7, s32[2,3]{1,0:T(2,128)} %bitcast.8, s32[768]{0:T(1024)} %kind_in.1, f32[128,768]{1,0:T(8,128)} %rhs_in.1, ...), custom_call_target="tpu_custom_call" | custom-call | tf_op jit(solution)/shard_map/pallas_call | solution.py:583
  94.8 0.9 shard_map.139

commit v3 on v2

--- a/solution.py
+++ b/solution.py
@@ -114,7 +114,7 @@
     col_offsets = [
         (dx, dl) for dx in range(X_SIZE) for dl in range(Z_LOW) if (dx, dl) != (0, 0)
     ]
-    col_offsets.sort(key=lambda o: -(ring_distance(o[0], X_SIZE) + (o[1] != 0)))
+    col_offsets.sort(key=lambda o: (o[1] == 0, -ring_distance(o[0], X_SIZE)))
 
     def plane_at(offset, sign):
         return shift(y, sign * offset[0], Y_SIZE), shift(core, sign * offset[1], CORES)
@@ -199,7 +199,7 @@
             + [(kind_in.at[block(q)], kind_ref.at[q]) for q in range(row_blocks)]
         )
     ]
-    for load in loads:
+    for load in loads[:3]:
         load.start()
     barrier = pltpu.get_barrier_semaphore()
     everyone = plane_to + z_to + cols_to
@@ -220,6 +220,8 @@
         return jnp.max(array.reshape(LANE // 8, 8, LANE), axis=0)
 
     loads[2].wait()
+    for load in loads[3:]:
+        load.start()
     col_best = [None] * col_blocks
     for q in range(row_blocks):
         across = None
@@ -408,7 +410,6 @@
     loads[4].wait()
     forward(x_start, 0)
     z_base = over_z(0, group_base)
-    first_bases = [over_cols(0, piece) for piece in range(pieces)]
     for load in loads[5:]:
         load.wait()
 
@@ -437,8 +438,7 @@
         put(x_full.at[own_group, :], x_full.at[own_group, :], y_base + k, device)
     put(x_full.at[own_group, :], x_full.at[own_group, :], relay_base + Y_SIZE - 1, partner)
 
-    for piece in range(pieces):
-        image_first[:, block(piece)] = image_sum(0, piece, first_bases[piece])
+    first_bases = [over_cols(0, piece) for piece in range(pieces)]
 
     for k in reversed(range(len(y_to))):
         rows = group_of(core, shift(y, -y_offsets[k], Y_SIZE))
@@ -450,8 +450,8 @@
 
     forward(x_full, 1)
     second_bases = [over_cols(1, piece) for piece in range(pieces)]
-    x_written = pltpu.make_async_copy(x_full, x_out, local.at[len(loads)])
-    x_written.start()
+    for piece in range(pieces):
+        image_first[:, block(piece)] = image_sum(0, piece, first_bases[piece])
 
     y_bases = []
     violations = products = moves = None
@@ -502,8 +502,6 @@
             arrived(target, y_bases[piece] + k, cols_to[k])
 
     half_base = backward(y_full, 1)
-    y_written = pltpu.make_async_copy(y_full, y_out, local.at[len(loads) + 1])
-    y_written.start()
     group_base = over_y(1, half_base)
     first_row = group * group_rows
     products = moves = None
@@ -519,6 +517,10 @@
     early_cols[column, 0:3, :] = added(y_sums, z_from, sums_base, z_to)
     early_base = share(early_cols, column, cols_to)
     z_base = over_z(1, group_base)
+    x_written = pltpu.make_async_copy(x_full, x_out, local.at[len(loads)])
+    x_written.start()
+    y_written = pltpu.make_async_copy(y_full, y_out, local.at[len(loads) + 1])
+    y_written.start()
     early_rows[group] = added(early_cols, cols_from, early_base, cols_to)
     early_base = share(early_rows, group, plane_to)
     summed = z_slots_in(high_slots.at[1], z_base)

time: 95.9 us -> 95.7 us (level)
  no operation moved by 1% of the time
where the time goes in v3:
time: 95.7 us; the launch traced here: 95.6 us
  Pallas kernels  94.9 us (99%)
    pallas_call x1, Pallas kernels, per_device(): pl.pallas_call(kernel, out_shape=(pltpu.VMEM((scenarios, cols_here), F32)...  94.1 us

profile of v3, /device:TPU:1, one launch (start us, length us, event | category | flops | bytes accessed | tf_op | source)
XLA Modules:
  0.0 95.6 jit_solution(6154954353412393862)
XLA Ops:
  0.6 94.1 %shard_map.138 = (f32[128,512]{1,0:T(8,128)S(1)}, f32[128,768]{1,0:T(8,128)S(1)}, f32[3,128]{1,0:T(4,128)S(1)}, f32[1,128]{1,0:T(1,128)S(1)}) custom-call(bf16[768,512]{1,0:T(8,128)(2,1)} %values_in.1, f32[2,3]{1,0:T(2,128)} %bitcast.7, s32[2,3]{1,0:T(2,128)} %bitcast.8, s32[768]{0:T(1024)} %kind_in.1, f32[128,768]{1,0:T(8,128)} %rhs_in.1, ...), custom_call_target="tpu_custom_call" | custom-call | tf_op jit(solution)/shard_map/pallas_call | solution.py:585
  94.7 0.9 shard_map.139
